TPU v7x, 32 devices: a whole 2x2x4 slice. The times are simulated.
32 devices in a mesh: gx: 4 (over y, x), gy: 8 (over z, core).
Axes of the slice: x: 2, y: 2, z: 4, core: 2. Of those that a mesh axis runs over, the one named last changes fastest.
Arguments:
- schur_blocks: float32 [32, 2048, 2048], P(('gx', 'gy')), may hold values from -1 to 11, as said below
- offsets: int32 [32], P(('gx', 'gy')), may hold values from 256 to 768, as said below
- right_side: float32 [32768, 128], P(('gx', 'gy')), may hold values from -20 to 20
- coarse_basis: float32 [32768, 128], P(('gx', 'gy')), may hold values from -0.03125 to 0.03125
- coarse_load: float32 [128, 128], replicated, may hold values from -6 to 6
Outputs:
- multipliers: float32 [32768, 128], P(('gx', 'gy'))
- amplitudes: float32 [128, 128], replicated
Inputs may be any that keep to these rules, and one draw needn't show every extreme that they name: `schur_blocks`: each block is symmetric positive definite. `offsets`: both ends of the range are taken by some subdomain.
All inputs are finite; a program needn't handle non-finite values.
Results may differ from a plain program's by a relative error of at most 0.0003.
Values sent between devices are 32-bit elements; how exact they have to be, the bound alone decides.
A program may use at most 128 MiB of HBM per device.

v0:
```python
import jax
import jax.numpy as jnp
from jax import lax
from jax.sharding import PartitionSpec as P

ITERS = 3


HIGHEST = lax.Precision.HIGHEST


def extended_2(block, sides, width):
    for axis, dim in sides:
        count = lax.axis_size(axis)
        forward = [(i, i + 1) for i in range(count - 1)]
        backward = [(target, source) for source, target in forward]
        low = lax.ppermute(
            lax.slice_in_dim(block, block.shape[dim] - width, None, axis=dim), axis, forward
        )
        high = lax.ppermute(lax.slice_in_dim(block, 0, width, axis=dim), axis, backward)
        block = jnp.concatenate([low, block, high], axis=dim)
    return block


def from_behind(value, axis, steps):
    count = lax.axis_size(axis)
    initial, last = (max(0, -steps), min(count, count - steps))
    return lax.ppermute(value, axis, [(source, source + steps) for source in range(initial, last)])


def apply_local(vector, schur_block, start_row):
    slab_rows = vector.shape[0]
    window_rows = schur_block.shape[0]
    extended = extended_2(vector, ((("gx", "gy"), 0),), slab_rows)
    window = lax.dynamic_slice_in_dim(extended, start_row, window_rows, 0)
    product_block = jnp.dot(
        schur_block, window, precision=HIGHEST, preferred_element_type=jnp.float32
    )
    spread = jnp.zeros((3 * slab_rows, vector.shape[1]), jnp.float32)
    spread = lax.dynamic_update_slice_in_dim(spread, product_block, start_row, 0)
    to_left = spread[:slab_rows]
    own_part = spread[slab_rows : 2 * slab_rows]
    to_right = spread[2 * slab_rows :]
    from_right = from_behind(to_left, ("gx", "gy"), -1)
    from_left = from_behind(to_right, ("gx", "gy"), 1)
    result = own_part + from_left + from_right
    return result


def project_sum(residual, coarse_basis, gram_factor):
    local_coarse = jnp.dot(
        coarse_basis.T, residual, precision=HIGHEST, preferred_element_type=jnp.float32
    )
    coarse_part, squares = lax.psum(
        (local_coarse, jnp.sum(residual * residual, axis=0)), ("gx", "gy")
    )
    amplitudes = jax.scipy.linalg.cho_solve((gram_factor, True), coarse_part)
    projected = residual - jnp.dot(
        coarse_basis, amplitudes, precision=HIGHEST, preferred_element_type=jnp.float32
    )
    energy = squares - jnp.sum(amplitudes * coarse_part, axis=0)
    return (projected, amplitudes, energy)


def local(schur_blocks, offsets, right_side, coarse_basis, coarse_load):
    schur_block = schur_blocks[0]
    start_row = offsets[0]
    local_gram = jnp.dot(
        coarse_basis.T, coarse_basis, precision=HIGHEST, preferred_element_type=jnp.float32
    )
    gram_matrix = lax.psum(local_gram, ("gx", "gy"))
    gram_factor = jnp.linalg.cholesky(gram_matrix)
    start_load = jax.scipy.linalg.cho_solve((gram_factor, True), coarse_load)
    multipliers = jnp.dot(
        coarse_basis, start_load, precision=HIGHEST, preferred_element_type=jnp.float32
    )
    residual = right_side - apply_local(multipliers, schur_block, start_row)
    projected, amplitudes, energy_now = project_sum(residual, coarse_basis, gram_factor)
    direction = projected
    for iteration in range(ITERS):
        operator_image = apply_local(direction, schur_block, start_row)
        curvature = lax.psum(jnp.sum(direction * operator_image, axis=0), ("gx", "gy"))
        step_length = energy_now / curvature
        multipliers = multipliers + step_length * direction
        residual = residual - step_length * operator_image
        projected, amplitudes, energy_next = project_sum(residual, coarse_basis, gram_factor)
        direction = projected + energy_next / energy_now * direction
        energy_now = energy_next
    return (multipliers, amplitudes)


def solution(mesh):
    in_specs = (
        P(("gx", "gy"), None, None),
        P(("gx", "gy")),
        P(("gx", "gy"), None),
        P(("gx", "gy"), None),
        P(),
    )
    out_specs = (P(("gx", "gy"), None), P())
    return jax.shard_map(local, mesh=mesh, in_specs=in_specs, out_specs=out_specs, check_vma=False)
```

profile of v0, /device:TPU:0, one launch (start us, length us, event | category | flops | bytes accessed | tf_op | source)
XLA Modules:
  0.0 1051.2 jit_solution(16787756393830020999)
XLA Ops:
  9.9 126.4 %all-reduce.7.cloned.1.call-done = f32[128,128]{0,1:T(8,128)} async-done(((f32[128,128]{0,1:T(8,128)}), f32[128,128]{0,1:T(8,128)}) %all-reduce.7.cloned.1.call-update) | async-done | bytes 65552 | tf_op jit(solution)/shard_map/psum | solution.py:71
  138.1 11.7 %cholesky.18 = f32[128,128]{1,0:T(8,128)S(1)} custom-call(f32[128,128]{1,0:T(8,128)S(1)} %fusion.66), custom_call_target="Cholesky" | custom-call | tf_op jit(solution)/shard_map/jit(cholesky)/cholesky | solution.py:72
  151.1 9.8 custom-call.12
  162.1 3.7 collective-permute-start
  170.3 20.9 %fusion.8 = f32[2048,128]{0,1:T(8,128)} fusion(f32[1,2048,2048]{2,1,0:T(8,128)} %param.7, s32[]{:T(128)S(6)} %select_n.7, f32[1024,128]{0,1:T(8,128)S(1)} %collective-permute-done, f32[1024,128]{0,1:T(8,128)S(1)} %convolution_bitcast_fusion.3, f32[1024,128]{0,1:T(8,128)S(1)} %collective-permute-done.1), kind=kOutput, calls=%fused_computation.8 | convolution fusion | flops 6442975232 | bytes 19398660 | tf_op jit(solution)/shard_map/dot_general | solution.py:36
  191.4 5.3 dynamic_update_slice.12
  199.0 14.0 %collective-permute-start.2 = (f32[1024,128]{0,1:T(8,128)}, f32[1024,128]{0,1:T(8,128)}, u32[]{:S(2)}, u32[]{:S(2)}) collective-permute-start(f32[1024,128]{0,1:T(8,128)} %get-tuple-element.25), channel_id=1, source_target_pairs={{0,1},{1,2},{2,3},{3,4},{4,5},{5,6},{6,7},{7,8},{8,9},{9,10},{10,1... | collective-permute-start | bytes 1572872 | tf_op jit(solution)/shard_map/ppermute | solution.py:28
  216.9 132.6 %all-reduce.9.cloned.1.call-done = f32[128,128]{0,1:T(8,128)} async-done(((f32[128,128]{0,1:T(8,128)}), f32[128,128]{0,1:T(8,128)}) %all-reduce.9.cloned.1.call-update) | async-done | bytes 65552 | tf_op jit(solution)/shard_map/psum | solution.py:54
  351.5 3.7 collective-permute-start.4
  356.6 3.1 collective-permute-done.5
  359.7 20.9 %fusion.11 = f32[2048,128]{0,1:T(8,128)} fusion(f32[1,2048,2048]{2,1,0:T(8,128)} %param.7, s32[]{:T(128)S(6)} %select_n.7, f32[1024,128]{0,1:T(8,128)S(1)} %collective-permute-done.4, f32[1024,128]{0,1:T(8,128)S(1)} %fusion.20, f32[1024,128]{0,1:T(8,128)S(1)} %collective-permute-done.5), kind=kOutput, calls=%fused_computation.9 | convolution fusion | flops 6442975232 | bytes 19398660 | tf_op jit(solution)/shard_map/dot_general | solution.py:36
  380.7 5.3 dynamic_update_slice.13
  388.4 14.0 %collective-permute-start.6 = (f32[1024,128]{0,1:T(8,128)}, f32[1024,128]{0,1:T(8,128)}, u32[]{:S(2)}, u32[]{:S(2)}) collective-permute-start(f32[1024,128]{0,1:T(8,128)} %get-tuple-element.23), channel_id=1, source_target_pairs={{0,1},{1,2},{2,3},{3,4},{4,5},{5,6},{6,7},{7,8},{8,9},{9,10},{10,1... | collective-permute-start | bytes 1572872 | tf_op jit(solution)/shard_map/ppermute | solution.py:28
  404.7 51.8 %all-reduce = (f32[128]{0:T(128)S(1)}, f32[128]{0:T(128)S(1)}) all-reduce(f32[128]{0:T(128)S(1)} %get-tuple-element.17, f32[128]{0:T(128)S(1)} %multiply_reduce_fusion.4), channel_id=1, replica_groups=mesh['gx'=4,'gy'=8] {'gx','gy'}, use_global_device_ids=true, to_apply=%region_4.6 | all-reduce | flops 256 | bytes 2048 | tf_op jit(solution)/shard_map/psum | solution.py:54
  459.5 41.2 %psum.81 = f32[128]{0:T(128)S(1)} all-reduce(f32[128]{0:T(128)S(1)} %get-tuple-element.13), channel_id=1, replica_groups=mesh['gx'=4,'gy'=8] {'gx','gy'}, use_global_device_ids=true, to_apply=%region_10.12 | all-reduce | flops 128 | bytes 1024 | tf_op jit(solution)/shard_map/psum | solution.py:54
  500.7 78.7 %all-reduce.11.cloned.1.call-done = f32[128,128]{0,1:T(8,128)} async-done(((f32[128,128]{0,1:T(8,128)}), f32[128,128]{0,1:T(8,128)}) %all-reduce.11.cloned.1.call-update) | async-done | bytes 65552 | tf_op jit(solution)/shard_map/psum | solution.py:54
  582.6 3.7 collective-permute-start.8
  587.7 3.1 collective-permute-done.9
  590.8 20.9 %fusion.14 = f32[2048,128]{0,1:T(8,128)} fusion(f32[1,2048,2048]{2,1,0:T(8,128)} %param.7, s32[]{:T(128)S(6)} %select_n.7, f32[1024,128]{0,1:T(8,128)S(1)} %collective-permute-done.8, f32[1024,128]{0,1:T(8,128)S(1)} %fusion.22, f32[1024,128]{0,1:T(8,128)S(1)} %collective-permute-done.9), kind=kOutput, calls=%fused_computation.10 | convolution fusion | flops 6442975232 | bytes 19398660 | tf_op jit(solution)/shard_map/dot_general | solution.py:36
  611.8 5.3 dynamic_update_slice.14
  618.5 13.2 %collective-permute-start.10 = (f32[1024,128]{0,1:T(8,128)S(1)}, f32[1024,128]{0,1:T(8,128)S(1)}, u32[]{:S(2)}, u32[]{:S(2)}) collective-permute-start(f32[1024,128]{0,1:T(8,128)S(1)} %get-tuple-element.21), channel_id=1, source_target_pairs={{0,1},{1,2},{2,3},{3,4},{4,5},{5,6},{6,7},{7,8},{8,9},{9,10},{10,1... | collective-permute-start | bytes 1572872 | tf_op jit(solution)/shard_map/ppermute | solution.py:28
  634.3 52.3 %psum.83 = f32[128]{0:T(128)S(1)} all-reduce(f32[128]{0:T(128)S(1)} %multiply_reduce_fusion.2), channel_id=1, replica_groups=mesh['gx'=4,'gy'=8] {'gx','gy'}, use_global_device_ids=true, to_apply=%region_14.16 | all-reduce | flops 128 | bytes 1024 | tf_op jit(solution)/shard_map/psum | solution.py:82
  691.3 40.7 %psum.84 = f32[128]{0:T(128)S(1)} all-reduce(f32[128]{0:T(128)S(1)} %get-tuple-element.9), channel_id=1, replica_groups=mesh['gx'=4,'gy'=8] {'gx','gy'}, use_global_device_ids=true, to_apply=%region_16.18 | all-reduce | flops 128 | bytes 1024 | tf_op jit(solution)/shard_map/psum | solution.py:54
  732.0 79.3 %all-reduce.13.cloned.1.call-done = f32[128,128]{0,1:T(8,128)} async-done(((f32[128,128]{0,1:T(8,128)}), f32[128,128]{0,1:T(8,128)}) %all-reduce.13.cloned.1.call-update) | async-done | bytes 65552 | tf_op jit(solution)/shard_map/psum | solution.py:54
  815.4 3.7 collective-permute-start.12
  820.6 3.0 collective-permute-done.13
  823.6 20.9 %fusion.17 = f32[2048,128]{0,1:T(8,128)} fusion(f32[1,2048,2048]{2,1,0:T(8,128)} %param.7, s32[]{:T(128)S(6)} %select_n.7, f32[1024,128]{0,1:T(8,128)S(1)} %collective-permute-done.12, f32[1024,128]{0,1:T(8,128)S(1)} %fusion.24, f32[1024,128]{0,1:T(8,128)S(1)} %collective-permute-done.13), kind=kOutput, calls=%fused_computation.11 | convolution fusion | flops 6442975232 | bytes 19398660 | tf_op jit(solution)/shard_map/dot_general | solution.py:36
  844.6 5.3 dynamic_update_slice.15
  851.5 13.2 %collective-permute-start.14 = (f32[1024,128]{0,1:T(8,128)S(1)}, f32[1024,128]{0,1:T(8,128)S(1)}, u32[]{:S(2)}, u32[]{:S(2)}) collective-permute-start(f32[1024,128]{0,1:T(8,128)S(1)} %get-tuple-element.19), channel_id=1, source_target_pairs={{0,1},{1,2},{2,3},{3,4},{4,5},{5,6},{6,7},{7,8},{8,9},{9,10},{10,1... | collective-permute-start | bytes 1572872 | tf_op jit(solution)/shard_map/ppermute | solution.py:28
  867.2 52.3 %psum.86 = f32[128]{0:T(128)S(1)} all-reduce(f32[128]{0:T(128)S(1)} %multiply_reduce_fusion), channel_id=1, replica_groups=mesh['gx'=4,'gy'=8] {'gx','gy'}, use_global_device_ids=true, to_apply=%region_20.22 | all-reduce | flops 128 | bytes 1024 | tf_op jit(solution)/shard_map/psum | solution.py:82
  919.6 2.7 convolution_bitcast_fusion.4
  924.7 117.6 %all-reduce.15.cloned.1.call-done = f32[128,128]{0,1:T(8,128)} async-done(((f32[128,128]{0,1:T(8,128)}), f32[128,128]{0,1:T(8,128)}) %all-reduce.15.cloned.1.call-update) | async-done | bytes 65552 | tf_op jit(solution)/shard_map/psum | solution.py:54
  (110 shorter events, 55.5 us)
Async XLA Ops:
  7.2 153.8 %copy-start.13 = (f32[128,128]{1,0:T(8,128)S(1)}, f32[128,128]{1,0:T(8,128)}, u32[]{:S(2)}) copy-start(f32[128,128]{1,0:T(8,128)} %param.11) | copy-start | bytes 196612
  7.2 129.1 %all-reduce.7.cloned.1.call-start = ((), (), s32[]{:S(2)}) async-start(), calls=%async_computation | async-start | bytes 131072 | tf_op jit(solution)/shard_map/psum | solution.py:71
  9.9 339.6 %all-reduce.9.cloned.1.call-start = ((), (), s32[]{:S(2)}) async-start(), calls=%async_computation.1 | async-start | bytes 131072 | tf_op jit(solution)/shard_map/psum | solution.py:54
  162.1 29.1 %copy-start.5 = (f32[1024,128]{0,1:T(8,128)}, f32[1024,128]{0,1:T(8,128)S(1)}, u32[]{:S(2)}) copy-start(f32[1024,128]{0,1:T(8,128)S(1)} %convolution_bitcast_fusion.3) | copy-start | bytes 1572868
  162.1 5.8 collective-permute-start
  165.8 4.6 collective-permute-start.1
  196.7 16.4 %copy-start.11 = (f32[1024,128]{1,0:T(8,128)S(1)}, f32[1024,128]{1,0:T(8,128)}, u32[]{:S(2)}) copy-start(f32[1024,128]{1,0:T(8,128)} %param.9) | copy-start | bytes 1572868
  197.8 15.5 %collective-permute-start.3 = (f32[1024,128]{0,1:T(8,128)}, f32[1024,128]{0,1:T(8,128)}, u32[]{:S(2)}, u32[]{:S(2)}) collective-permute-start(f32[1024,128]{0,1:T(8,128)} %get-tuple-element.26), channel_id=1, source_target_pairs={{1,0},{2,1},{3,2},{4,3},{5,4},{6,5},{7,6},{8,7},{9,8},{10,9},{11,1... | collective-permute-start | bytes 1572872 | tf_op jit(solution)/shard_map/ppermute | solution.py:28
  199.0 15.1 %collective-permute-start.2 = (f32[1024,128]{0,1:T(8,128)}, f32[1024,128]{0,1:T(8,128)}, u32[]{:S(2)}, u32[]{:S(2)}) collective-permute-start(f32[1024,128]{0,1:T(8,128)} %get-tuple-element.25), channel_id=1, source_target_pairs={{0,1},{1,2},{2,3},{3,4},{4,5},{5,6},{6,7},{7,8},{8,9},{9,10},{10,1... | collective-permute-start | bytes 1572872 | tf_op jit(solution)/shard_map/ppermute | solution.py:28
  215.5 136.0 %copy-start.4 = (f32[1024,128]{0,1:T(8,128)}, f32[1024,128]{0,1:T(8,128)S(1)}, u32[]{:S(2)}) copy-start(f32[1024,128]{0,1:T(8,128)S(1)} %get-tuple-element.18) | copy-start | bytes 1572868
  216.8 362.7 %all-reduce.11.cloned.1.call-start = ((), (), s32[]{:S(2)}) async-start(), calls=%async_computation.2 | async-start | bytes 131072 | tf_op jit(solution)/shard_map/psum | solution.py:54
  351.5 5.1 collective-permute-start.4
  355.1 4.6 collective-permute-start.5
  386.1 16.5 %copy-start.12 = (f32[128,128]{0,1:T(8,128)S(1)}, f32[128,128]{0,1:T(8,128)}, u32[]{:S(2)}) copy-start(f32[128,128]{0,1:T(8,128)} %all-reduce.9.cloned.1.call-done) | copy-start | bytes 196612
  387.1 15.5 %collective-permute-start.7 = (f32[1024,128]{0,1:T(8,128)}, f32[1024,128]{0,1:T(8,128)S(1)}, u32[]{:S(2)}, u32[]{:S(2)}) collective-permute-start(f32[1024,128]{0,1:T(8,128)} %get-tuple-element.24), channel_id=1, source_target_pairs={{1,0},{2,1},{3,2},{4,3},{5,4},{6,5},{7,6},{8,7},{9,8},{10,9},{11,1... | collective-permute-start | bytes 1572872 | tf_op jit(solution)/shard_map/ppermute | solution.py:28
  388.4 15.1 %collective-permute-start.6 = (f32[1024,128]{0,1:T(8,128)}, f32[1024,128]{0,1:T(8,128)}, u32[]{:S(2)}, u32[]{:S(2)}) collective-permute-start(f32[1024,128]{0,1:T(8,128)} %get-tuple-element.23), channel_id=1, source_target_pairs={{0,1},{1,2},{2,3},{3,4},{4,5},{5,6},{6,7},{7,8},{8,9},{9,10},{10,1... | collective-permute-start | bytes 1572872 | tf_op jit(solution)/shard_map/ppermute | solution.py:28
  402.7 53.9 %copy-start.6 = (f32[1024,128]{0,1:T(8,128)}, f32[1024,128]{0,1:T(8,128)S(1)}, u32[]{:S(2)}) copy-start(f32[1024,128]{0,1:T(8,128)S(1)} %collective-permute-done.7) | copy-start | bytes 1572868
  458.1 124.4 %copy-start.1 = (f32[1024,128]{0,1:T(8,128)}, f32[1024,128]{0,1:T(8,128)S(1)}, u32[]{:S(2)}) copy-start(f32[1024,128]{0,1:T(8,128)S(1)} %get-tuple-element.14) | copy-start | bytes 1572868
  459.5 351.8 %all-reduce.13.cloned.1.call-start = ((), (), s32[]{:S(2)}) async-start(), calls=%async_computation.3 | async-start | bytes 131072 | tf_op jit(solution)/shard_map/psum | solution.py:54
  582.6 5.1 collective-permute-start.8
  586.2 4.6 collective-permute-start.9
  617.2 14.6 %collective-permute-start.11 = (f32[1024,128]{0,1:T(8,128)S(1)}, f32[1024,128]{0,1:T(8,128)S(1)}, u32[]{:S(2)}, u32[]{:S(2)}) collective-permute-start(f32[1024,128]{0,1:T(8,128)S(1)} %get-tuple-element.22), channel_id=1, source_target_pairs={{1,0},{2,1},{3,2},{4,3},{5,4},{6,5},{7,6},{8,7},{9,8},{10,9},{11,1... | collective-permute-start | bytes 1572872 | tf_op jit(solution)/shard_map/ppermute | solution.py:28
  618.5 14.7 %collective-permute-start.10 = (f32[1024,128]{0,1:T(8,128)S(1)}, f32[1024,128]{0,1:T(8,128)S(1)}, u32[]{:S(2)}, u32[]{:S(2)}) collective-permute-start(f32[1024,128]{0,1:T(8,128)S(1)} %get-tuple-element.21), channel_id=1, source_target_pairs={{0,1},{1,2},{2,3},{3,4},{4,5},{5,6},{6,7},{7,8},{8,9},{9,10},{10,1... | collective-permute-start | bytes 1572872 | tf_op jit(solution)/shard_map/ppermute | solution.py:28
  631.8 1.5 copy-start.7
  691.3 351.0 %all-reduce.15.cloned.1.call-start = ((), (), s32[]{:S(2)}) async-start(), calls=%async_computation.4 | async-start | bytes 131072 | tf_op jit(solution)/shard_map/psum | solution.py:54
  815.4 29.1 %copy-start.2 = (f32[1024,128]{0,1:T(8,128)}, f32[1024,128]{0,1:T(8,128)S(1)}, u32[]{:S(2)}) copy-start(f32[1024,128]{0,1:T(8,128)S(1)} %fusion.24) | copy-start | bytes 1572868
  815.4 5.2 collective-permute-start.12
  819.0 4.6 collective-permute-start.13
  850.0 17.1 %copy-start.3 = (f32[1024,128]{0,1:T(8,128)S(1)}, f32[1024,128]{0,1:T(8,128)}, u32[]{:S(2)}) copy-start(f32[1024,128]{0,1:T(8,128)} %copy-done.2) | copy-start | bytes 1572868
  850.1 14.7 %collective-permute-start.15 = (f32[1024,128]{0,1:T(8,128)S(1)}, f32[1024,128]{0,1:T(8,128)S(1)}, u32[]{:S(2)}, u32[]{:S(2)}) collective-permute-start(f32[1024,128]{0,1:T(8,128)S(1)} %get-tuple-element.20), channel_id=1, source_target_pairs={{1,0},{2,1},{3,2},{4,3},{5,4},{6,5},{7,6},{8,7},{9,8},{10,9},{11,1... | collective-permute-start | bytes 1572872 | tf_op jit(solution)/shard_map/ppermute | solution.py:28
  851.5 14.7 %collective-permute-start.14 = (f32[1024,128]{0,1:T(8,128)S(1)}, f32[1024,128]{0,1:T(8,128)S(1)}, u32[]{:S(2)}, u32[]{:S(2)}) collective-permute-start(f32[1024,128]{0,1:T(8,128)S(1)} %get-tuple-element.19), channel_id=1, source_target_pairs={{0,1},{1,2},{2,3},{3,4},{4,5},{5,6},{6,7},{7,8},{8,9},{9,10},{10,1... | collective-permute-start | bytes 1572872 | tf_op jit(solution)/shard_map/ppermute | solution.py:28
  864.8 1.5 copy-start.9
  (3 other events, 2.7 us)
Sparse Core Ops, SparseCore 0:
  14.1 122.0 all-reduce.6
  216.9 132.4 all-reduce.8
  459.6 119.8 all-reduce.10
  691.4 119.8 all-reduce.12
  922.5 119.8 all-reduce.14
where the time goes:
time: 1060 us; the launch traced here: 1050 us
  waiting for transfers between devices  551 us (52%)
  blocking collectives  238 us (22%)
  matrix products  103 us (10%)
  starting transfers between devices  80.2 us (8%)
  other arithmetic  34 us (3%)
  local copies, waits for them, and re-layouts  29.1 us (3%)
  between operations  15.5 us (1%)
    psum x4, waiting for transfers between devices, project_sum(): lax.psum((local_coarse, jnp.sum(residual * residual, axis=0)), ('gx', 'gy'))  408 us
    psum x3, blocking collectives, project_sum(): lax.psum((local_coarse, jnp.sum(residual * residual, axis=0)), ('gx', 'gy'))  134 us
    psum x1, waiting for transfers between devices, local(): gram_matrix = lax.psum(local_gram, ('gx', 'gy'))  126 us
    psum x2, blocking collectives, local(): lax.psum(jnp.sum(direction * operator_image, axis=0), ('gx', 'gy'))  105 us
    dot_general x4, matrix products, apply_local(): jnp.dot(schur_block, window, precision=HIGHEST, preferred_element_type=jn...  83.5 us
    ppermute x8, starting transfers between devices, from_behind(): lax.ppermute(value, axis, [(source, source + steps) for source in range(i...  59.8 us
    dynamic_update_slice x4, local copies, waits for them, and re-layouts, apply_local(): lax.dynamic_update_slice_in_dim(spread, product_block, start_row, 0)  21.3 us
  transfers between devices with their start and end apart: 21, of which 15 were waited for; matrix products, arithmetic and copies ran while one was open for 0% of the time, Pallas kernels for 0%

commit v1 on v0

v1 whole, which is shorter than its diff:
```python
import functools

import jax
import jax.numpy as jnp
from jax import lax
from jax.experimental import pallas as pl
from jax.experimental.pallas import tpu as pltpu
from jax.sharding import PartitionSpec as P

ITERS = 3
MESH = pl.DeviceIdType.MESH
HIGHEST = lax.Precision.HIGHEST
F32 = jnp.float32
BF16 = jnp.bfloat16
CHUNK = 128
SLOTS = 4
BLOCK = 512
EXCHANGES = 2 * ITERS + 2
REDUCES = 2 + ITERS


def dot(a, b):
    return jnp.dot(a, b, precision=HIGHEST, preferred_element_type=F32)


def kernel(
    nx, ny, off_ref, schur_ref, right_ref, basis_ref, load_ref, lam_ref, amp_ref,
    stage, s_hi, s_lo, vec, twice, basis_w, basis_t, fc_own, fc_w, fc_t, right_w, z, d, p_old, image_old, own,
    out_l, out_r, in_l, in_r, part, fold, total, m_ref, sweep, scal_in, scal_all,
    stage_sem, hs_l, hs_r, hr_l, hr_r, fold_s, fold_r, tot_s, tot_r, scal_s, scal_r,
):
    n = nx * ny
    slab = right_ref.shape[0]
    nc = basis_ref.shape[1]
    width = 2 * slab
    low = slab // 4
    span = slab - low
    me = lax.axis_index("gx") * ny + lax.axis_index("gy")
    off = off_ref[0]
    chunks = width // CHUNK

    def where_is(i):
        return (lax.div(i, ny), lax.rem(i, ny))

    def fetch(i, slot):
        return pltpu.make_async_copy(
            schur_ref.at[pl.ds(i * CHUNK, CHUNK), :], stage.at[slot], stage_sem.at[slot]
        )

    for i in range(SLOTS):
        fetch(i, i).start()

    @pl.when(me == 0)
    def _():
        in_l[...] = jnp.zeros_like(in_l)

    @pl.when(me == n - 1)
    def _():
        in_r[...] = jnp.zeros_like(in_r)

    barrier = pltpu.get_barrier_semaphore()

    def greet(k, carry):
        pl.semaphore_signal(barrier, inc=1, device_id=where_is(lax.rem(me + k, n)), device_id_type=MESH)
        return carry

    lax.fori_loop(1, n, greet, 0)
    pl.semaphore_wait(barrier, n - 1)

    def to_right(e, src):
        return pltpu.make_async_remote_copy(
            src_ref=src, dst_ref=in_l.at[e], send_sem=hs_r.at[e], recv_sem=hr_l.at[e],
            device_id=where_is(lax.rem(me + 1, n)), device_id_type=MESH,
        )

    def to_left(e, src):
        return pltpu.make_async_remote_copy(
            src_ref=src, dst_ref=in_r.at[e], send_sem=hs_l.at[e], recv_sem=hr_r.at[e],
            device_id=where_is(lax.rem(me + n - 1, n)), device_id_type=MESH,
        )

    def send_halo(e, src_l, src_r):
        @pl.when(me > 0)
        def _():
            to_left(e, src_l).start()

        @pl.when(me < n - 1)
        def _():
            to_right(e, src_r).start()

    def wait_halo(e):
        @pl.when(me > 0)
        def _():
            to_right(e, out_r.at[0]).wait_recv()

        @pl.when(me < n - 1)
        def _():
            to_left(e, out_l.at[0]).wait_recv()

    def wait_sent(e):
        @pl.when(me > 0)
        def _():
            to_left(e, out_l.at[0]).wait_send()

        @pl.when(me < n - 1)
        def _():
            to_right(e, out_r.at[0]).wait_send()

    def rows_below(first, count):
        return lax.broadcasted_iota(jnp.int32, (count, nc), 0) + first < off

    def folded_halo(e, first, count):
        mask = rows_below(first, count)
        right = in_r[e, pl.ds(first, count), :] if first + count <= span else jnp.zeros((count, nc), F32)
        left = in_l[e, pl.ds(first - low, count), :] if first >= low else jnp.zeros((count, nc), F32)
        return jnp.where(mask, right, left)

    def folded(e):
        return jnp.concatenate([folded_halo(e, i * low, low) for i in range(slab // low)], axis=0)

    def apply_block(src):
        twice[0:width, :] = src[...]
        twice[width:, :] = src[...]
        window = twice[pl.ds(off, width), :]
        hi = window.astype(BF16)
        vec[:, :nc] = hi
        vec[:, nc:] = (window - hi.astype(F32)).astype(BF16)

        def rows(i, carry):
            at = pl.ds(pl.multiple_of(i * BLOCK, BLOCK), BLOCK)
            both = jnp.dot(s_hi[at, :], vec[...], preferred_element_type=F32)
            rest = jnp.dot(s_lo[at, :], vec[:, :nc], preferred_element_type=F32)
            result = both[:, :nc] + (both[:, nc:] + rest)
            twice[at, :] = result
            twice[pl.ds(pl.multiple_of(width + i * BLOCK, BLOCK), BLOCK), :] = result
            return carry

        lax.fori_loop(0, width // BLOCK, rows, 0)

    def folded_product():
        return twice[pl.ds(width - off, width), :]

    def send_parts(e, k, product):
        mask = rows_below(0, slab)
        head = product[:slab]
        out_l[k] = jnp.where(mask, 0.0, head)[low:]
        out_r[k] = jnp.where(mask, head, 0.0)[:span]
        send_halo(e, out_l.at[k], out_r.at[k])

    def assemble(e, product):
        wait_halo(e)
        left = in_l[e]
        right = in_r[e]
        mine = product[slab:]
        return jnp.concatenate(
            [
                mine[:low] + left[:low],
                mine[low:span] + (left[low:] + right[: span - low]),
                mine[span:] + right[span - low :],
            ],
            axis=0,
        )

    def reduce_start(r, value):
        rows = value.shape[0]
        p = rows // n
        for i in range(n):
            part[r][i] = value[i * p : (i + 1) * p]

        def send(k, carry):
            peer = lax.rem(me + k, n)
            pltpu.make_async_remote_copy(
                src_ref=part[r].at[peer], dst_ref=fold[r].at[me], send_sem=fold_s.at[r],
                recv_sem=fold_r.at[r], device_id=where_is(peer), device_id_type=MESH,
            ).start()
            return carry

        lax.fori_loop(1, n, send, 0)
        fold[r][me] = part[r][me]

    def reduce_turn(r):
        arrived = fold[r].at[pl.ds(0, n - 1)]
        pltpu.make_async_copy(arrived, arrived, fold_r.at[r]).wait()
        total[r][me] = jnp.sum(fold[r][...], axis=0)

        def send(k, carry):
            peer = lax.rem(me + k, n)
            pltpu.make_async_remote_copy(
                src_ref=total[r].at[me], dst_ref=total[r].at[me], send_sem=tot_s.at[r],
                recv_sem=tot_r.at[r], device_id=where_is(peer), device_id_type=MESH,
            ).start()
            return carry

        lax.fori_loop(1, n, send, 0)

    def reduce_end(r):
        arrived = total[r].at[pl.ds(0, n - 1)]
        pltpu.make_async_copy(arrived, arrived, tot_r.at[r]).wait()
        p = total[r].shape[1]
        for i in range(n):
            m_ref[i * p : (i + 1) * p, :] = total[r][i]
        return m_ref[: n * p, :]

    def scal_start(it):
        scal_all[it, me] = scal_in[it]

        def send(k, carry):
            peer = lax.rem(me + k, n)
            pltpu.make_async_remote_copy(
                src_ref=scal_in.at[it], dst_ref=scal_all.at[it, me], send_sem=scal_s.at[it],
                recv_sem=scal_r.at[it], device_id=where_is(peer), device_id_type=MESH,
            ).start()
            return carry

        lax.fori_loop(1, n, send, 0)

    def scal_end(it):
        arrived = scal_all.at[it, pl.ds(0, n - 1)]
        pltpu.make_async_copy(arrived, arrived, scal_r.at[it]).wait()
        sums = jnp.sum(scal_all[it], axis=0)
        return sums[0:1], sums[1:2], sums[2:3]

    send_halo(0, basis_ref.at[pl.ds(0, span)], basis_ref.at[pl.ds(low, span)])
    send_halo(1, right_ref.at[pl.ds(0, span)], right_ref.at[pl.ds(low, span)])
    basis_t[...] = basis_ref[...].T
    both = jnp.concatenate([basis_ref[...], right_ref[...]], axis=1)
    local = dot(basis_t[...], both)
    reduce_start(0, jnp.concatenate([local[:, :nc], local[:, nc:]], axis=0))

    def split(i, carry):
        slot = lax.rem(i, SLOTS)
        fetch(i, slot).wait()
        at = pl.ds(pl.multiple_of(i * CHUNK, CHUNK), CHUNK)
        value = stage[slot]
        hi = value.astype(BF16)
        s_hi[at, :] = hi
        s_lo[at, :] = (value - hi.astype(F32)).astype(BF16)

        @pl.when(i + SLOTS < chunks)
        def _():
            fetch(i + SLOTS, slot).start()

        return carry

    lax.fori_loop(0, chunks, split, 0)
    reduce_turn(0)

    wait_halo(0)
    basis_w[0:slab, :] = folded(0)
    basis_w[slab:, :] = basis_ref[...]
    apply_block(basis_w)
    product = folded_product()
    send_parts(2, 0, product)
    fc_own[...] = assemble(2, product)
    send_halo(3, fc_own.at[pl.ds(0, span)], fc_own.at[pl.ds(low, span)])
    reduce_start(1, dot(basis_t[...], fc_own[...]))
    fc_t[...] = fc_own[...].T
    gram = reduce_end(0)
    sweep[...] = gram[:nc]
    right_coarse = gram[nc:]
    reduce_turn(1)

    lanes = lax.broadcasted_iota(jnp.int32, (nc, nc), 1)
    subs = lax.broadcasted_iota(jnp.int32, (nc, nc), 0)

    def pivot(k, a):
        row = sweep[pl.ds(k, 1), :]
        here = lanes == k
        col = jnp.sum(jnp.where(here, a, 0.0), axis=1, keepdims=True)
        inverse = 1.0 / jnp.sum(jnp.where(lanes[:1] == k, row, 0.0), axis=1, keepdims=True)
        scaled = row * inverse
        new = a - col * scaled
        new = jnp.where(here, col * inverse, new)
        new = jnp.where(subs == k, jnp.where(here, -inverse, scaled), new)
        sweep[...] = new
        return new

    ginv = -lax.fori_loop(0, nc, pivot, sweep[...])

    y0 = dot(ginv, load_ref[...])
    lam_ref[...] = dot(basis_ref[...], y0)
    cfc = reduce_end(1)
    amp = dot(ginv, right_coarse - dot(cfc, y0))
    wait_halo(1)
    wait_halo(3)
    right_w[0:slab, :] = folded(1)
    right_w[slab:, :] = right_ref[...]
    fc_w[0:slab, :] = folded(3)
    fc_w[slab:, :] = fc_own[...]
    z[...] = right_w[...] - dot(fc_w[...], y0) - dot(basis_w[...], amp)

    energy = curvature = coarse_image = None
    for it in range(ITERS):
        last = it == ITERS - 1
        reduce_start(2 + it, dot(fc_t[...], z[slab:, :]))
        apply_block(z)
        product = folded_product()
        e = 4 + 2 * it
        if not last:
            send_parts(e, 1 + it, product)
        scal_in[it, 0:1] = jnp.sum(z[...] * product, axis=0, keepdims=True)
        scal_in[it, 1:2] = jnp.sum(z[slab:, :] * z[slab:, :], axis=0, keepdims=True)
        if it == 0:
            scal_in[it, 2:3] = jnp.zeros((1, nc), F32)
        else:
            scal_in[it, 2:3] = jnp.sum(z[...] * p_old[...], axis=0, keepdims=True)
        scal_in[it, 3:4] = jnp.zeros((1, nc), F32)
        scal_start(it)
        reduce_turn(2 + it)
        if not last:
            own[it] = assemble(e, product)
            send_halo(e + 1, own.at[it, pl.ds(0, span)], own.at[it, pl.ds(low, span)])
        curved, energy_now, crossed = scal_end(it)
        coarse_now = reduce_end(2 + it)
        if it == 0:
            d[...] = z[slab:, :]
            curvature = curved
            coarse_image = coarse_now
            if not last:
                p_old[...] = product
        else:
            beta = energy_now / energy
            d[...] = z[slab:, :] + beta * d[...]
            curvature = curved + beta * (2.0 * crossed + beta * curvature)
            coarse_image = coarse_now + beta * coarse_image
            if not last:
                p_old[...] = product + beta * p_old[...]
        energy = energy_now
        step = energy / curvature
        lam_ref[...] += step * d[...]
        shift = dot(ginv, coarse_image)
        amp = amp - step * shift
        if not last:
            wait_halo(e + 1)
            whole = jnp.concatenate([folded(e + 1), own[it]], axis=0)
            if it > 0:
                whole = whole + beta * image_old[...]
            image_old[...] = whole
            z[...] = z[...] - step * (whole - dot(basis_w[...], shift))
    amp_ref[...] = amp

    for e in range(EXCHANGES):
        wait_sent(e)
    for r in range(REDUCES):
        sent = fold[r].at[pl.ds(0, n - 1)]
        pltpu.make_async_copy(sent, sent, fold_s.at[r]).wait()
        sent = total[r].at[pl.ds(0, n - 1)]
        pltpu.make_async_copy(sent, sent, tot_s.at[r]).wait()
    for it in range(ITERS):
        sent = scal_all.at[it, pl.ds(0, n - 1)]
        pltpu.make_async_copy(sent, sent, scal_s.at[it]).wait()


def entry(nx, ny, groups, *refs):
    fixed = refs[: groups[0]]
    rest = refs[groups[0] :]
    part, rest = rest[:REDUCES], rest[REDUCES:]
    fold, rest = rest[:REDUCES], rest[REDUCES:]
    total, rest = rest[:REDUCES], rest[REDUCES:]
    kernel(nx, ny, *fixed, part, fold, total, *rest)


def solution(mesh):
    nx, ny = mesh.shape["gx"], mesh.shape["gy"]
    n = nx * ny

    def local(schur_blocks, offsets, right_side, coarse_basis, coarse_load):
        slab, r = right_side.shape
        nc = coarse_basis.shape[1]
        width = schur_blocks.shape[1]
        span = slab - slab // 4
        row_counts = [2 * nc] + [nc] * (REDUCES - 1)

        def pieces():
            return [pltpu.VMEM((n, rows // n, r), F32) for rows in row_counts]

        vmem = pl.BlockSpec(memory_space=pltpu.VMEM)
        fixed = [
            pltpu.VMEM((SLOTS, CHUNK, width), F32),
            pltpu.VMEM((width, width), BF16),
            pltpu.VMEM((width, width), BF16),
            pltpu.VMEM((width, 2 * r), BF16),
            pltpu.VMEM((2 * width, r), F32),
            pltpu.VMEM((width, nc), F32),
            pltpu.VMEM((nc, slab), F32),
            pltpu.VMEM((slab, nc), F32),
            pltpu.VMEM((width, nc), F32),
            pltpu.VMEM((nc, slab), F32),
            pltpu.VMEM((width, r), F32),
            pltpu.VMEM((width, r), F32),
            pltpu.VMEM((slab, r), F32),
            pltpu.VMEM((width, r), F32),
            pltpu.VMEM((width, r), F32),
            pltpu.VMEM((ITERS - 1, slab, r), F32),
            pltpu.VMEM((ITERS, span, r), F32),
            pltpu.VMEM((ITERS, span, r), F32),
            pltpu.VMEM((EXCHANGES, span, r), F32),
            pltpu.VMEM((EXCHANGES, span, r), F32),
        ]
        dma = pltpu.SemaphoreType.DMA
        rest = [
            pltpu.VMEM((2 * nc, r), F32),
            pltpu.VMEM((nc, nc), F32),
            pltpu.VMEM((ITERS, 4, r), F32),
            pltpu.VMEM((ITERS, n, 4, r), F32),
            dma((SLOTS,)),
            dma((EXCHANGES,)), dma((EXCHANGES,)), dma((EXCHANGES,)), dma((EXCHANGES,)),
            dma((REDUCES,)), dma((REDUCES,)), dma((REDUCES,)), dma((REDUCES,)),
            dma((ITERS,)), dma((ITERS,)),
        ]
        return pl.pallas_call(
            functools.partial(entry, nx, ny, (7 + len(fixed),)),
            out_shape=(
                jax.ShapeDtypeStruct((slab, r), F32),
                jax.ShapeDtypeStruct((nc, r), F32),
            ),
            in_specs=[
                pl.BlockSpec(memory_space=pltpu.SMEM),
                pl.BlockSpec(memory_space=pl.ANY),
                vmem, vmem, vmem,
            ],
            out_specs=(vmem, vmem),
            scratch_shapes=fixed + pieces() + pieces() + pieces() + rest,
            compiler_params=pltpu.CompilerParams(
                collective_id=0, has_side_effects=True, vmem_limit_bytes=60 * 1024 * 1024
            ),
            name="projected_cg",
        )(offsets, schur_blocks[0], right_side, coarse_basis, coarse_load)

    in_specs = (
        P(("gx", "gy"), None, None),
        P(("gx", "gy")),
        P(("gx", "gy"), None),
        P(("gx", "gy"), None),
        P(),
    )
    out_specs = (P(("gx", "gy"), None), P())
    return jax.shard_map(local, mesh=mesh, in_specs=in_specs, out_specs=out_specs, check_vma=False)
```

time: 1060 us -> 157 us (0.15)
  waiting for transfers between devices: 551 us -> 0 us
  blocking collectives: 238 us -> 0 us
  Pallas kernels: 0 us -> 152 us
  matrix products: 103 us -> 0 us
  starting transfers between devices: 80.2 us -> 0 us
  other arithmetic: 34 us -> 0 us
  local copies, waits for them, and re-layouts: 29.1 us -> 3.34 us
  between operations: 15.5 us -> 1.29 us
    psum x5 -> x0, waiting for transfers between devices: 535 us -> none  [the longest x4 408 us: project_sum(): lax.psum((local_coarse, jnp.sum(residual * residual, axis=0)), ('gx', 'gy'))]
    psum x5 -> x0, blocking collectives: 238 us -> none  [the longest x3 134 us: project_sum(): lax.psum((local_coarse, jnp.sum(residual * residual, axis=0)), ('gx', 'gy'))]
    pallas_call x0 -> x1, Pallas kernels: none -> 152 us  [local(): pl.pallas_call(functools.partial(entry, nx, ny, (7 + len(fixed),)), out_s...]
    dot_general x13 -> x0, matrix products: 96.4 us -> none  [the longest x4 83.5 us: apply_local(): jnp.dot(schur_block, window, precision=HIGHEST, preferred_element_type=jn...]
    ppermute x16 -> x0, starting transfers between devices: 80 us -> none  [the longest x8 59.8 us: from_behind(): lax.ppermute(value, axis, [(source, source + steps) for source in range(i...]
    another operation x5 -> x0, other arithmetic: 22.9 us -> none  [the longest x3 12.4 us: local(): gram_factor = jnp.linalg.cholesky(gram_matrix)]
    dynamic_update_slice x4 -> x0, local copies, waits for them, and re-layouts: 21.3 us -> none  [apply_local(): lax.dynamic_update_slice_in_dim(spread, product_block, start_row, 0)]
    ppermute x16 -> x0, waiting for transfers between devices: 16.5 us -> none  [the longest x4 11.6 us: extended_2(): lax.ppermute(lax.slice_in_dim(block, 0, width, axis=dim), axis, backward)]
  transfers between devices with their start and end apart: 21 -> 0, of which waited for: 15 -> 0; matrix products, arithmetic and copies ran while one was open for 0% -> 0% of each run, Pallas kernels for 0% -> 0%
where the time goes in v1:
time: 157 us; the launch traced here: 156 us
  Pallas kernels  152 us (97%)
  local copies, waits for them, and re-layouts  3.34 us (2%)
    pallas_call x1, Pallas kernels, local(): pl.pallas_call(functools.partial(entry, nx, ny, (7 + len(fixed),)), out_s...  152 us
    unnamed x2, local copies, waits for them, and re-layouts  3.34 us

profile of v1, /device:TPU:0, one launch (start us, length us, event | category | flops | bytes accessed | tf_op | source)
XLA Modules:
  0.0 156.4 jit_solution(15149682668044009799)
XLA Ops:
  1.3 151.8 %projected_cg.1 = (f32[1024,128]{1,0:T(8,128)}, f32[128,128]{1,0:T(8,128)}) custom-call(s32[1]{0:T(128)S(6)} %copy.9.refs_0_, f32[2048,2048]{1,0:T(8,128)} %bitcast.1, f32[1024,128]{1,0:T(8,128)} %refs_2_.1, f32[1024,128]{1,0:T(8,128)} %refs_3_.1, f32[128,128]{1,0:T(8,128)} %refs_4_.1), custom_call_target="tpu_custom_call" | custom-call | tf_op jit(solution)/shard_map/projected_cg/pallas_call | solution.py:411
  153.0 1.9 %copy.10 = f32[1024,128]{1,0:T(8,128)} copy(f32[1024,128]{1,0:T(8,128)} %get-tuple-element.4) | data formatting | bytes 1048576
  154.9 1.5 copy.11

commit v2 on v1

--- a/solution.py
+++ b/solution.py
@@ -221,7 +221,6 @@
         return sums[0:1], sums[1:2], sums[2:3]
 
     send_halo(0, basis_ref.at[pl.ds(0, span)], basis_ref.at[pl.ds(low, span)])
-    send_halo(1, right_ref.at[pl.ds(0, span)], right_ref.at[pl.ds(low, span)])
     basis_t[...] = basis_ref[...].T
     both = jnp.concatenate([basis_ref[...], right_ref[...]], axis=1)
     local = dot(basis_t[...], both)
@@ -259,23 +258,37 @@
     sweep[...] = gram[:nc]
     right_coarse = gram[nc:]
     reduce_turn(1)
+    send_halo(1, right_ref.at[pl.ds(0, span)], right_ref.at[pl.ds(low, span)])
 
     lanes = lax.broadcasted_iota(jnp.int32, (nc, nc), 1)
     subs = lax.broadcasted_iota(jnp.int32, (nc, nc), 0)
 
-    def pivot(k, a):
-        row = sweep[pl.ds(k, 1), :]
+    def eliminate(a, k, row, col, p):
         here = lanes == k
-        col = jnp.sum(jnp.where(here, a, 0.0), axis=1, keepdims=True)
-        inverse = 1.0 / jnp.sum(jnp.where(lanes[:1] == k, row, 0.0), axis=1, keepdims=True)
+        inverse = 1.0 / p
         scaled = row * inverse
         new = a - col * scaled
         new = jnp.where(here, col * inverse, new)
-        new = jnp.where(subs == k, jnp.where(here, -inverse, scaled), new)
-        sweep[...] = new
-        return new
-
-    ginv = -lax.fori_loop(0, nc, pivot, sweep[...])
+        return jnp.where(subs == k, jnp.where(here, -inverse, scaled), new), scaled, inverse
+
+    def pick(row, k):
+        return jnp.sum(jnp.where(lanes[:1] == k, row, 0.0), axis=1, keepdims=True)
+
+    def pivot(half, a):
+        k = 2 * half
+        row1, row2 = sweep[pl.ds(k, 1), :], sweep[pl.ds(k + 1, 1), :]
+        col1 = jnp.sum(jnp.where(lanes == k, a, 0.0), axis=1, keepdims=True)
+        col2 = jnp.sum(jnp.where(lanes == k + 1, a, 0.0), axis=1, keepdims=True)
+        p1, cross, p2 = pick(row1, k), pick(row1, k + 1), pick(row2, k + 1)
+        a, scaled, inverse = eliminate(a, k, row1, col1, p1)
+        ratio = cross * inverse
+        row2 = jnp.where(lanes[:1] == k, ratio, row2 - cross * scaled)
+        col2 = jnp.where(subs[:, :1] == k, ratio, col2 - col1 * ratio)
+        a, _, _ = eliminate(a, k + 1, row2, col2, p2 - cross * ratio)
+        sweep[...] = a
+        return a
+
+    ginv = -lax.fori_loop(0, nc // 2, pivot, sweep[...])
 
     y0 = dot(ginv, load_ref[...])
     lam_ref[...] = dot(basis_ref[...], y0)

time: 157 us -> 144 us (0.917)
  Pallas kernels: 152 us -> 139 us
    pallas_call x1, Pallas kernels: 152 us -> 139 us  [local(): pl.pallas_call(functools.partial(entry, nx, ny, (7 + len(fixed),)), out_s...]
where the time goes in v2:
time: 144 us
  Pallas kernels  139 us (97%)
  local copies, waits for them, and re-layouts  3.34 us (2%)
    pallas_call x1, Pallas kernels, local(): pl.pallas_call(functools.partial(entry, nx, ny, (7 + len(fixed),)), out_s...  139 us
    unnamed x2, local copies, waits for them, and re-layouts  3.34 us

profile of v2, /device:TPU:0, one launch (start us, length us, event | category | flops | bytes accessed | tf_op | source)
XLA Modules:
  0.0 143.5 jit_solution(14047215585919979602)
XLA Ops:
  1.3 138.9 %projected_cg.1 = (f32[1024,128]{1,0:T(8,128)}, f32[128,128]{1,0:T(8,128)}) custom-call(s32[1]{0:T(128)S(6)} %copy.9.refs_0_, f32[2048,2048]{1,0:T(8,128)} %bitcast.1, f32[1024,128]{1,0:T(8,128)} %refs_2_.1, f32[1024,128]{1,0:T(8,128)} %refs_3_.1, f32[128,128]{1,0:T(8,128)} %refs_4_.1), custom_call_target="tpu_custom_call" | custom-call | tf_op jit(solution)/shard_map/projected_cg/pallas_call | solution.py:424
  140.2 1.9 %copy.10 = f32[1024,128]{1,0:T(8,128)} copy(f32[1024,128]{1,0:T(8,128)} %get-tuple-element.4) | data formatting | bytes 1048576
  142.0 1.5 %copy.11 = f32[128,128]{1,0:T(8,128)} copy(f32[128,128]{1,0:T(8,128)} %get-tuple-element.5) | data formatting | bytes 131072
